TPU v7x, 32 devices: a whole 2x2x4 slice. The times are simulated.
32 devices in a mesh: wide: 8 (over z, y), narrow: 4 (over x, core).
Axes of the slice: x: 2, y: 2, z: 4, core: 2. Of those that a mesh axis runs over, the one named last changes fastest.
Arguments:
- tokens: bfloat16 [32, 256, 1024], P(('wide', 'narrow')), may hold values from -6 to 6
- segment_ids: int32 [32, 256], P(('wide', 'narrow')), may hold values from 0 to 3, never falling along the last dimension, each value on 1 to 128 neighbouring positions
- routed_index: int32 [32, 32], P(('wide', 'narrow')), may hold values from 0 to 255, as said below
- out_grad: bfloat16 [32, 256, 1024], P(('wide', 'narrow')), may hold values from -6 to 6
- dense_attn_gain: bfloat16 [1024], P('wide'), may hold values from 0.5 to 1.5
- dense_qkv: bfloat16 [1024, 3072], P('wide'), may hold values from -0.1875 to 0.1875
- dense_proj: bfloat16 [1024, 1024], P('wide'), may hold values from -0.75 to 0.75
- dense_mlp_gain: bfloat16 [1024], P('wide'), may hold values from 0.5 to 1.5
- dense_up: bfloat16 [1024, 4096], P('wide'), may hold values from -0.1875 to 0.1875
- dense_down: bfloat16 [4096, 1024], P('wide'), may hold values from -0.09375 to 0.09375
- routed_attn_gain: bfloat16 [1024], P('wide'), may hold values from 0.5 to 1.5
- routed_qkv: bfloat16 [1024, 3072], P('wide'), may hold values from -0.1875 to 0.1875
- routed_proj: bfloat16 [1024, 1024], P('wide'), may hold values from -0.75 to 0.75
- routed_mlp_gain: bfloat16 [1024], P('wide'), may hold values from 0.5 to 1.5
- routed_up: bfloat16 [1024, 4096], P('wide'), may hold values from -0.1875 to 0.1875
- routed_down: bfloat16 [4096, 1024], P('wide'), may hold values from -0.09375 to 0.09375
- router_vector: bfloat16 [1024], replicated, may hold values from -0.1875 to 0.1875
Outputs:
- result: bfloat16 [32, 256, 1024], P(('wide', 'narrow'))
- input_grad: bfloat16 [32, 256, 1024], P(('wide', 'narrow'))
- grad_dense_attn_gain: float32 [1024], P('wide')
- grad_dense_qkv: float32 [1024, 3072], P('wide')
- grad_dense_proj: float32 [1024, 1024], P('wide')
- grad_dense_mlp_gain: float32 [1024], P('wide')
- grad_dense_up: float32 [1024, 4096], P('wide')
- grad_dense_down: float32 [4096, 1024], P('wide')
- grad_routed_attn_gain: float32 [1024], P('wide')
- grad_routed_qkv: float32 [1024, 3072], P('wide')
- grad_routed_proj: float32 [1024, 1024], P('wide')
- grad_routed_mlp_gain: float32 [1024], P('wide')
- grad_routed_up: float32 [1024, 4096], P('wide')
- grad_routed_down: float32 [4096, 1024], P('wide')
- router_grad: float32 [1024], replicated
Inputs may be any that keep to these rules, and one draw needn't show every extreme that they name: `routed_index`: each row holds 32 distinct positions of its sequence in increasing order.
All inputs are finite; a program needn't handle non-finite values.
Results may differ from a plain program's by a relative error of at most 0.022.
Values may be sent and summed in bfloat16 or wider, within the bound.
No kernel may reach another device: no remote copies, remote signals or barrier semaphores. Data moves between devices by JAX's collectives and lax.ppermute only.
A program may use at most 256 MiB of HBM per device.

v0:
```python
import jax
import jax.numpy as jnp
from jax import lax
from jax.sharding import PartitionSpec as P

HEADS = 16
EPS = 1e-06
NEG = -1e30
HIGH = lax.Precision.HIGHEST
GROUP_HEADS = 4


def rms_norm(values, gain):
    return values * lax.rsqrt(jnp.mean(values * values, -1, keepdims=True) + EPS) * gain


def gelu_tanh(values):
    return jax.nn.gelu(values, approximate=True)


def row_dot(left, right):
    return jnp.dot(left, right, preferred_element_type=jnp.float32)


def cross_dot(left, right):
    return lax.dot_general(
        left, right, (((0,), (0,)), ((), ())), preferred_element_type=jnp.float32
    )


def back_dot(left, right):
    return lax.dot_general(
        left, right, (((1,), (1,)), ((), ())), preferred_element_type=jnp.float32
    )


def block_mask(query_pos, query_seg, key_pos, key_seg):
    return (key_pos[None, :] <= query_pos[:, None]) & (key_seg[None, :] == query_seg[:, None])


def attend_forward(queries, key_rows, val_rows, positions, segments):
    row_count, head_count, head_width = queries.shape
    block_rows = min(512, row_count)
    block_count = row_count // block_rows
    score_scale = head_width ** (-0.5)
    group_size = min(GROUP_HEADS, head_count)

    def one_block(packed):
        query_blk, query_pos, query_seg = packed
        allowed = block_mask(query_pos, query_seg, positions, segments)[None]
        outputs = []
        logsums = []
        for head_start in range(0, head_count, group_size):
            head_slice = slice(head_start, head_start + group_size)
            scores = (
                jnp.einsum(
                    "qhd,khd->hqk",
                    query_blk[:, head_slice],
                    key_rows[:, head_slice],
                    preferred_element_type=jnp.float32,
                )
                * score_scale
            )
            scores = jnp.where(allowed, scores, NEG)
            highest = jnp.max(scores, -1, keepdims=True)
            lifted = jnp.exp(scores - highest)
            summed = jnp.sum(lifted, -1, keepdims=True)
            attn_prob = (lifted / summed).astype(jnp.bfloat16)
            outputs.append(
                jnp.einsum(
                    "hqk,khd->qhd",
                    attn_prob,
                    val_rows[:, head_slice],
                    preferred_element_type=jnp.float32,
                )
            )
            logsums.append((highest + jnp.log(summed))[:, :, 0])
        return (jnp.concatenate(outputs, 1), jnp.concatenate(logsums, 0))

    stacked = (
        queries.reshape(block_count, block_rows, head_count, head_width),
        positions.reshape(block_count, block_rows),
        segments.reshape(block_count, block_rows),
    )
    output, logsum = lax.map(one_block, stacked)
    return (output.reshape(row_count, head_count, head_width), logsum)


def attend_backward(queries, key_rows, val_rows, positions, segments, logsum, output_grad):
    row_count, head_count, head_width = queries.shape
    block_rows = min(512, row_count)
    block_count = row_count // block_rows
    score_scale = head_width ** (-0.5)
    group_size = min(GROUP_HEADS, head_count)

    def one_block(carry, packed):
        key_grad, val_grad = carry
        query_blk, query_pos, query_seg, logsum_blk, grad_blk = packed
        allowed = block_mask(query_pos, query_seg, positions, segments)[None]
        query_parts = []
        key_parts = []
        val_parts = []
        for head_start in range(0, head_count, group_size):
            head_slice = slice(head_start, head_start + group_size)
            scores = (
                jnp.einsum(
                    "qhd,khd->hqk",
                    query_blk[:, head_slice],
                    key_rows[:, head_slice],
                    preferred_element_type=jnp.float32,
                )
                * score_scale
            )
            scores = jnp.where(allowed, scores, NEG)
            attn_prob = jnp.exp(scores - logsum_blk[head_slice][:, :, None])
            prob_grad = jnp.einsum(
                "qhd,khd->hqk",
                grad_blk[:, head_slice],
                val_rows[:, head_slice],
                preferred_element_type=jnp.float32,
            )
            row_inner = jnp.sum(attn_prob * prob_grad, -1, keepdims=True)
            score_grad = (attn_prob * (prob_grad - row_inner)).astype(jnp.bfloat16)
            query_parts.append(
                jnp.einsum(
                    "hqk,khd->qhd",
                    score_grad,
                    key_rows[:, head_slice],
                    preferred_element_type=jnp.float32,
                )
                * score_scale
            )
            key_parts.append(
                jnp.einsum(
                    "hqk,qhd->khd",
                    score_grad,
                    query_blk[:, head_slice],
                    preferred_element_type=jnp.float32,
                )
                * score_scale
            )
            val_parts.append(
                jnp.einsum(
                    "hqk,qhd->khd",
                    attn_prob.astype(jnp.bfloat16),
                    grad_blk[:, head_slice],
                    preferred_element_type=jnp.float32,
                )
            )
        updated = (
            key_grad + jnp.concatenate(key_parts, 1),
            val_grad + jnp.concatenate(val_parts, 1),
        )
        return (updated, jnp.concatenate(query_parts, 1))

    zero_grad = jnp.zeros(key_rows.shape, jnp.float32)
    stacked = (
        queries.reshape(block_count, block_rows, head_count, head_width),
        positions.reshape(block_count, block_rows),
        segments.reshape(block_count, block_rows),
        logsum,
        output_grad.reshape(block_count, block_rows, head_count, head_width),
    )
    (key_grad, val_grad), query_grad = lax.scan(one_block, (zero_grad, zero_grad), stacked)
    return (query_grad.reshape(row_count, head_count, head_width), key_grad, val_grad)


def attend_layer(inputs, gain, mixing, project, positions, segments):
    row_count, model_width = inputs.shape
    normed, norm_back = jax.vjp(rms_norm, inputs, gain)
    normed_low = normed.astype(jnp.bfloat16)
    combined = row_dot(normed_low, mixing).astype(jnp.bfloat16)
    parts = combined.reshape(row_count, 3, HEADS, model_width // HEADS)
    queries = parts[:, 0]
    key_rows = parts[:, 1]
    val_rows = parts[:, 2]
    output, logsum = attend_forward(queries, key_rows, val_rows, positions, segments)
    output_low = output.reshape(row_count, model_width).astype(jnp.bfloat16)
    branch = row_dot(output_low, project)
    return (branch, (norm_back, normed_low, queries, key_rows, val_rows, logsum, output_low))


def attend_layer_back(branch_grad, kept, mixing, project, positions, segments):
    norm_back, normed_low, queries, key_rows, val_rows, logsum, output_low = kept
    row_count = output_low.shape[0]
    grad_low = branch_grad.astype(jnp.bfloat16)
    project_grad = cross_dot(output_low, grad_low)
    output_grad = back_dot(grad_low, project).astype(jnp.bfloat16)
    query_grad, key_grad, val_grad = attend_backward(
        queries, key_rows, val_rows, positions, segments, logsum, output_grad.reshape(queries.shape)
    )
    combined_grad = (
        jnp.stack([query_grad, key_grad, val_grad], 1).reshape(row_count, -1).astype(jnp.bfloat16)
    )
    mixing_grad = cross_dot(normed_low, combined_grad)
    input_grad, gain_grad = norm_back(back_dot(combined_grad, mixing))
    return (input_grad, gain_grad, mixing_grad, project_grad)


def feed_layer(inputs, gain, upward, downward):
    normed, norm_back = jax.vjp(rms_norm, inputs, gain)
    normed_low = normed.astype(jnp.bfloat16)
    hidden_pre = row_dot(normed_low, upward)
    active, gelu_back = jax.vjp(gelu_tanh, hidden_pre)
    active_low = active.astype(jnp.bfloat16)
    return (row_dot(active_low, downward), (norm_back, normed_low, gelu_back, active_low))


def feed_layer_back(branch_grad, kept, upward, downward):
    norm_back, normed_low, gelu_back, active_low = kept
    grad_low = branch_grad.astype(jnp.bfloat16)
    down_grad = cross_dot(active_low, grad_low)
    active_grad = back_dot(grad_low, downward)
    pre_grad = gelu_back(active_grad)[0].astype(jnp.bfloat16)
    up_grad = cross_dot(normed_low, pre_grad)
    input_grad, gain_grad = norm_back(back_dot(pre_grad, upward))
    return (input_grad, gain_grad, up_grad, down_grad)


def fetch_weights(weights):
    attn_gain, mixing, project, feed_gain, upward, downward = weights
    return (
        lax.all_gather(attn_gain, "wide", axis=0, tiled=True),
        lax.all_gather(mixing, "wide", axis=0, tiled=True),
        lax.all_gather(project, "wide", axis=0, tiled=True),
        lax.all_gather(feed_gain, "wide", axis=0, tiled=True),
        lax.all_gather(upward, "wide", axis=0, tiled=True),
        lax.all_gather(downward, "wide", axis=0, tiled=True),
    )


def reduce_grads(grads):
    attn_gain, mixing, project, feed_gain, upward, downward = grads
    shares = (
        lax.psum_scatter(
            attn_gain.astype(jnp.bfloat16), "wide", scatter_dimension=0, tiled=True
        ).astype(jnp.float32),
        lax.psum_scatter(
            mixing.astype(jnp.bfloat16), "wide", scatter_dimension=0, tiled=True
        ).astype(jnp.float32),
        lax.psum_scatter(
            project.astype(jnp.bfloat16), "wide", scatter_dimension=0, tiled=True
        ).astype(jnp.float32),
        lax.psum_scatter(
            feed_gain.astype(jnp.bfloat16), "wide", scatter_dimension=0, tiled=True
        ).astype(jnp.float32),
        lax.psum_scatter(
            upward.astype(jnp.bfloat16), "wide", scatter_dimension=0, tiled=True
        ).astype(jnp.float32),
        lax.psum_scatter(
            downward.astype(jnp.bfloat16), "wide", scatter_dimension=0, tiled=True
        ).astype(jnp.float32),
    )
    return (
        lax.psum(shares[0].astype(jnp.bfloat16), "narrow").astype(jnp.float32),
        lax.psum(shares[1].astype(jnp.bfloat16), "narrow").astype(jnp.float32),
        lax.psum(shares[2].astype(jnp.bfloat16), "narrow").astype(jnp.float32),
        lax.psum(shares[3].astype(jnp.bfloat16), "narrow").astype(jnp.float32),
        lax.psum(shares[4].astype(jnp.bfloat16), "narrow").astype(jnp.float32),
        lax.psum(shares[5].astype(jnp.bfloat16), "narrow").astype(jnp.float32),
    )


def per_device(
    tokens,
    segment_ids,
    routed_index,
    out_grad,
    dense_attn_gain,
    dense_qkv,
    dense_proj,
    dense_mlp_gain,
    dense_up,
    dense_down,
    routed_attn_gain,
    routed_qkv,
    routed_proj,
    routed_mlp_gain,
    routed_up,
    routed_down,
    router_vector,
):
    inputs = tokens[0].astype(jnp.float32)
    segments = segment_ids[0]
    chosen = routed_index[0]
    positions = jnp.arange(inputs.shape[0], dtype=jnp.int32)
    dense_full = fetch_weights(
        (dense_attn_gain, dense_qkv, dense_proj, dense_mlp_gain, dense_up, dense_down)
    )
    routed_full = fetch_weights(
        (routed_attn_gain, routed_qkv, routed_proj, routed_mlp_gain, routed_up, routed_down)
    )
    dense_att, dense_kept_att = attend_layer(
        inputs, dense_full[0].astype(jnp.float32), dense_full[1], dense_full[2], positions, segments
    )
    hidden = inputs + dense_att
    dense_ffn, dense_kept_ffn = feed_layer(
        hidden, dense_full[3].astype(jnp.float32), dense_full[4], dense_full[5]
    )
    middle = hidden + dense_ffn
    selected = jnp.take(middle, chosen, axis=0)
    chosen_seg = jnp.take(segments, chosen)
    route_vec = router_vector.astype(jnp.float32)
    rate = jax.nn.sigmoid(jnp.dot(selected, route_vec, precision=HIGH))
    routed_att, routed_kept_att = attend_layer(
        selected,
        routed_full[0].astype(jnp.float32),
        routed_full[1],
        routed_full[2],
        chosen,
        chosen_seg,
    )
    after_att = selected + routed_att
    routed_ffn, routed_kept_ffn = feed_layer(
        after_att, routed_full[3].astype(jnp.float32), routed_full[4], routed_full[5]
    )
    change = routed_att + routed_ffn
    result = middle.at[chosen].add(rate[:, None] * change)
    result_grad = out_grad[0].astype(jnp.float32)
    picked_grad = jnp.take(result_grad, chosen, axis=0)
    rate_grad = jnp.sum(picked_grad * change, -1)
    change_grad = rate[:, None] * picked_grad
    logit_grad = rate_grad * rate * (1.0 - rate)
    after_grad, routed_feed_gain_grad, routed_up_grad, routed_down_grad = feed_layer_back(
        change_grad, routed_kept_ffn, routed_full[4], routed_full[5]
    )
    att_in_grad, routed_attn_gain_grad, routed_qkv_grad, routed_proj_grad = attend_layer_back(
        change_grad + after_grad,
        routed_kept_att,
        routed_full[1],
        routed_full[2],
        chosen,
        chosen_seg,
    )
    selected_grad = after_grad + att_in_grad + logit_grad[:, None] * route_vec[None, :]
    router_local = jnp.dot(logit_grad, selected, precision=HIGH)
    routed_grads = reduce_grads(
        (
            routed_attn_gain_grad,
            routed_qkv_grad,
            routed_proj_grad,
            routed_feed_gain_grad,
            routed_up_grad,
            routed_down_grad,
        )
    )
    router_total = lax.psum(router_local, ("wide", "narrow"))
    middle_grad = result_grad.at[chosen].add(selected_grad)
    hidden_in_grad, dense_feed_gain_grad, dense_up_grad, dense_down_grad = feed_layer_back(
        middle_grad, dense_kept_ffn, dense_full[4], dense_full[5]
    )
    hidden_grad = middle_grad + hidden_in_grad
    input_part, dense_attn_gain_grad, dense_qkv_grad, dense_proj_grad = attend_layer_back(
        hidden_grad, dense_kept_att, dense_full[1], dense_full[2], positions, segments
    )
    input_total = hidden_grad + input_part
    dense_grads = reduce_grads(
        (
            dense_attn_gain_grad,
            dense_qkv_grad,
            dense_proj_grad,
            dense_feed_gain_grad,
            dense_up_grad,
            dense_down_grad,
        )
    )
    return (
        result.astype(jnp.bfloat16)[None],
        input_total.astype(jnp.bfloat16)[None],
        dense_grads[0],
        dense_grads[1],
        dense_grads[2],
        dense_grads[3],
        dense_grads[4],
        dense_grads[5],
        routed_grads[0],
        routed_grads[1],
        routed_grads[2],
        routed_grads[3],
        routed_grads[4],
        routed_grads[5],
        router_total,
    )


def solution(mesh):
    return jax.shard_map(
        per_device,
        mesh=mesh,
        in_specs=(
            P(("wide", "narrow"), None, None),
            P(("wide", "narrow"), None),
            P(("wide", "narrow"), None),
            P(("wide", "narrow"), None, None),
            P("wide"),
            P("wide", None),
            P("wide", None),
            P("wide"),
            P("wide", None),
            P("wide", None),
            P("wide"),
            P("wide", None),
            P("wide", None),
            P("wide"),
            P("wide", None),
            P("wide", None),
            P(),
        ),
        out_specs=(
            P(("wide", "narrow"), None, None),
            P(("wide", "narrow"), None, None),
            P("wide"),
            P("wide", None),
            P("wide", None),
            P("wide"),
            P("wide", None),
            P("wide", None),
            P("wide"),
            P("wide", None),
            P("wide", None),
            P("wide"),
            P("wide", None),
            P("wide", None),
            P(),
        ),
        check_vma=False,
    )
```

profile of v0, /device:TPU:0, one launch (start us, length us, event | category | flops | bytes accessed | tf_op | source)
XLA Modules:
  0.0 1981.9 jit_solution(2973243669548970490)
XLA Ops:
  14.0 22.8 %all-gather = bf16[8,1,128]{2,1,0:T(2,128)(2,1)S(1)} all-gather(bf16[1,1,128]{2,1,0:T(2,128)(2,1)S(1)} %bitcast.332), channel_id=1, replica_groups=mesh['wide'=8,'narrow'=4] {'wide'}, dimensions={0}, use_global_device_ids=true | all-gather | bytes 2304 | tf_op jit(solution)/shard_map/all_gather | solution.py:223
  36.8 16.9 all-gather.1
  53.7 18.9 all-gather.2
  72.5 16.9 all-gather.3
  92.5 19.4 all-gather.13.cloned.1.call-done
  111.9 5.8 convolution_convert_fusion.6
  124.2 37.1 %all-gather.15.cloned.1.call-done = bf16[1024,1024]{1,0:T(8,128)(2,1)} async-done(((bf16[128,1024]{1,0:T(8,128)(2,1)}), bf16[1024,1024]{1,0:T(8,128)(2,1)}) %all-gather.15.cloned.1.call-update) | async-done | bytes 2097168 | tf_op jit(solution)/shard_map/all_gather | solution.py:225
  161.4 2.4 multiply_reduce_fusion.6
  163.8 122.7 %all-gather.17.cloned.1.call-done = bf16[1024,4096]{1,0:T(8,128)(2,1)} async-done(((bf16[128,4096]{1,0:T(8,128)(2,1)}), bf16[1024,4096]{1,0:T(8,128)(2,1)}) %all-gather.17.cloned.1.call-update) | async-done | bytes 8388624 | tf_op jit(solution)/shard_map/all_gather | solution.py:227
  286.5 7.8 fusion.211
  294.3 116.9 %all-gather.19.cloned.1.call-done = bf16[4096,1024]{1,0:T(8,128)(2,1)} async-done(((bf16[512,1024]{1,0:T(8,128)(2,1)}), bf16[4096,1024]{1,0:T(8,128)(2,1)}) %all-gather.19.cloned.1.call-update) | async-done | bytes 8388624 | tf_op jit(solution)/shard_map/all_gather | solution.py:228
  411.2 7.4 convolution_add_fusion.1
  419.5 90.7 %all-gather.21.cloned.1.call-done = bf16[1024,3072]{1,0:T(8,128)(2,1)} async-done(((bf16[128,3072]{1,0:T(8,128)(2,1)}), bf16[1024,3072]{1,0:T(8,128)(2,1)}) %all-gather.21.cloned.1.call-update) | async-done | bytes 6291472 | tf_op jit(solution)/shard_map/all_gather | solution.py:224
  510.2 4.0 convolution_convert_fusion.7
  516.6 43.1 %all-gather.23.cloned.1.call-done = bf16[1024,1024]{1,0:T(8,128)(2,1)} async-done(((bf16[128,1024]{1,0:T(8,128)(2,1)}), bf16[1024,1024]{1,0:T(8,128)(2,1)}) %all-gather.23.cloned.1.call-update) | async-done | bytes 2097168 | tf_op jit(solution)/shard_map/all_gather | solution.py:225
  559.7 2.8 multiply_reduce_fusion.12
  562.8 122.0 %all-gather.25.cloned.1.call-done = bf16[1024,4096]{1,0:T(8,128)(2,1)} async-done(((bf16[128,4096]{1,0:T(8,128)(2,1)}), bf16[1024,4096]{1,0:T(8,128)(2,1)}) %all-gather.25.cloned.1.call-update) | async-done | bytes 8388624 | tf_op jit(solution)/shard_map/all_gather | solution.py:227
  684.8 5.2 fusion.205
  690.0 119.6 %all-gather.27.cloned.1.call-done = bf16[4096,1024]{1,0:T(8,128)(2,1)} async-done(((bf16[512,1024]{1,0:T(8,128)(2,1)}), bf16[4096,1024]{1,0:T(8,128)(2,1)}) %all-gather.27.cloned.1.call-update) | async-done | bytes 8388624 | tf_op jit(solution)/shard_map/all_gather | solution.py:228
  809.6 6.2 fusion.84
  815.9 3.2 multiply_reduce_fusion.7
  826.0 5.1 convolution_add_fusion.2
  831.2 3.2 multiply_reduce_fusion.8
  834.4 4.0 scatter_custom_fusion.1
  838.4 9.3 fusion.6
  847.8 7.3 multiply_reduce_fusion
  874.7 3.1 multiply_reduce_fusion.2
  888.1 4.6 convolution_convert_fusion.5
  893.7 4.5 convolution_convert_fusion.4
  898.8 7.3 convolution_convert_fusion.3
  907.4 8.4 convolution_convert_fusion.2
  916.8 5.7 convolution_convert_fusion.1
  923.6 5.6 convolution_convert_fusion
  929.3 66.9 %reduce-scatter.19.cloned.1.call-done = bf16[128,1024]{1,0:T(8,128)(2,1)} async-done(((bf16[1024,1024]{1,0:T(8,128)(2,1)}), bf16[128,1024]{1,0:T(8,128)(2,1)}) %reduce-scatter.19.cloned.1.call-update) | async-done | bytes 262160 | tf_op jit(solution)/shard_map/reduce_scatter | solution.py:241
  996.3 120.7 %reduce-scatter.9.cloned.1.call-done = bf16[128,3072]{1,0:T(8,128)(2,1)} async-done(((bf16[1024,3072]{1,0:T(8,128)(2,1)}), bf16[128,3072]{1,0:T(8,128)(2,1)}) %reduce-scatter.9.cloned.1.call-update) | async-done | bytes 786448 | tf_op jit(solution)/shard_map/reduce_scatter | solution.py:238
  1116.9 120.8 %reduce-scatter.17.cloned.1.call-done = bf16[128,3072]{1,0:T(8,128)(2,1)} async-done(((bf16[1024,3072]{1,0:T(8,128)(2,1)}), bf16[128,3072]{1,0:T(8,128)(2,1)}) %reduce-scatter.17.cloned.1.call-update) | async-done | bytes 786448 | tf_op jit(solution)/shard_map/reduce_scatter | solution.py:238
  1237.7 150.3 %reduce-scatter.13.cloned.1.call-done = bf16[128,4096]{1,0:T(8,128)(2,1)} async-done(((bf16[1024,4096]{1,0:T(8,128)(2,1)}), bf16[128,4096]{1,0:T(8,128)(2,1)}) %reduce-scatter.13.cloned.1.call-update) | async-done | bytes 1048592 | tf_op jit(solution)/shard_map/reduce_scatter | solution.py:247
  1388.0 150.1 %reduce-scatter.15.cloned.1.call-done = bf16[512,1024]{1,0:T(8,128)(2,1)} async-done(((bf16[4096,1024]{1,0:T(8,128)(2,1)}), bf16[512,1024]{1,0:T(8,128)(2,1)}) %reduce-scatter.15.cloned.1.call-update) | async-done | bytes 1048592 | tf_op jit(solution)/shard_map/reduce_scatter | solution.py:250
  1538.1 150.1 %reduce-scatter.21.cloned.1.call-done = bf16[128,4096]{1,0:T(8,128)(2,1)} async-done(((bf16[1024,4096]{1,0:T(8,128)(2,1)}), bf16[128,4096]{1,0:T(8,128)(2,1)}) %reduce-scatter.21.cloned.1.call-update) | async-done | bytes 1048592 | tf_op jit(solution)/shard_map/reduce_scatter | solution.py:247
  1688.2 150.1 %reduce-scatter.23.cloned.1.call-done = bf16[512,1024]{1,0:T(8,128)(2,1)} async-done(((bf16[4096,1024]{1,0:T(8,128)(2,1)}), bf16[512,1024]{1,0:T(8,128)(2,1)}) %reduce-scatter.23.cloned.1.call-update) | async-done | bytes 1048592 | tf_op jit(solution)/shard_map/reduce_scatter | solution.py:250
  1841.0 6.2 fusion.62
  1847.2 19.7 all-reduce.4
  1867.3 6.5 all-reduce.5
  1876.0 37.8 %psum.103 = f32[1024]{0:T(1024)} all-reduce(f32[1024]{0:T(1024)S(1)} %bitcast.330), channel_id=1, replica_groups=mesh['wide'=8,'narrow'=4] {'wide','narrow'}, use_global_device_ids=true, to_apply=%region_63.65 | all-reduce | flops 1024 | bytes 8192 | tf_op jit(solution)/shard_map/psum | solution.py:347
  1914.7 2.3 fusion.89
  1917.1 44.0 %all-reduce.9.cloned.1.call-done = (bf16[128,3072]{1,0:T(8,128)(2,1)}, bf16[128,1024]{1,0:T(8,128)(2,1)}, bf16[128,4096]{1,0:T(8,128)(2,1)}, bf16[512,1024]{1,0:...) async-done(((bf16[128,3072]{1,0:T(8,128)(2,1)}, bf16[128,1024]{1,0:T(8,128)(2,1)}, ...) | async-done | bytes 6291472 | tf_op jit(solution)/shard_map/psum | solution.py:256
  1961.1 2.6 convert_element_type.368
  1965.5 2.9 convert_element_type.374
  (399 shorter events, 74.6 us)
Async XLA Ops:
  7.2 29.6 %copy-start.101 = (bf16[128]{0:T(256)(128)(2,1)S(1)}, bf16[128]{0:T(256)(128)(2,1)}, u32[]{:S(2)}) copy-start(bf16[128]{0:T(256)(128)(2,1)} %param.26) | copy-start | bytes 772
  7.2 46.4 %copy-start.102 = (bf16[128]{0:T(256)(128)(2,1)S(1)}, bf16[128]{0:T(256)(128)(2,1)}, u32[]{:S(2)}) copy-start(bf16[128]{0:T(256)(128)(2,1)} %param.29) | copy-start | bytes 772
  7.2 65.3 %copy-start.103 = (bf16[128]{0:T(256)(128)(2,1)S(1)}, bf16[128]{0:T(256)(128)(2,1)}, u32[]{:S(2)}) copy-start(bf16[128]{0:T(256)(128)(2,1)} %param.32) | copy-start | bytes 772
  7.2 82.2 %copy-start.92 = (s32[1,32]{1,0:T(1,128)S(1)}, s32[1,32]{1,0:T(1,128)}, u32[]{:S(2)}) copy-start(s32[1,32]{1,0:T(1,128)} %param.21) | copy-start | bytes 388
  7.2 82.7 %copy-start = (s32[1,256]{1,0:T(1,128)S(1)}, s32[1,256]{1,0:T(1,128)}, u32[]{:S(2)}) copy-start(s32[1,256]{1,0:T(1,128)} %param.20) | copy-start | bytes 3076
  7.3 83.4 %copy-start.42 = (bf16[1,256,1024]{2,1,0:T(8,128)(2,1)S(1)}, bf16[1,256,1024]{2,1,0:T(8,128)(2,1)}, u32[]{:S(2)}) copy-start(bf16[1,256,1024]{2,1,0:T(8,128)(2,1)} %param.22) | copy-start | bytes 1572868
  7.3 104.6 %all-gather.13.cloned.1.call-start = ((), (), s32[]{:S(2)}) async-start(), calls=%async_computation.8 | async-start | bytes 7077888 | tf_op jit(solution)/shard_map/all_gather | solution.py:224
  8.0 153.4 %all-gather.15.cloned.1.call-start = ((), (), s32[]{:S(2)}) async-start(), calls=%async_computation.9 | async-start | bytes 2359296 | tf_op jit(solution)/shard_map/all_gather | solution.py:225
  8.7 82.7 %copy-start.12 = (bf16[1,256,1024]{2,1,0:T(8,128)(2,1)S(1)}, bf16[1,256,1024]{2,1,0:T(8,128)(2,1)}, u32[]{:S(2)}) copy-start(bf16[1,256,1024]{2,1,0:T(8,128)(2,1)} %param.19) | copy-start | bytes 1572868
  8.8 277.8 %all-gather.17.cloned.1.call-start = ((), (), s32[]{:S(2)}) async-start(), calls=%async_computation.10 | async-start | bytes 9437184 | tf_op jit(solution)/shard_map/all_gather | solution.py:227
  9.5 401.7 %all-gather.19.cloned.1.call-start = ((), (), s32[]{:S(2)}) async-start(), calls=%async_computation.11 | async-start | bytes 9437184 | tf_op jit(solution)/shard_map/all_gather | solution.py:228
  10.1 500.1 %all-gather.21.cloned.1.call-start = ((), (), s32[]{:S(2)}) async-start(), calls=%async_computation.12 | async-start | bytes 7077888 | tf_op jit(solution)/shard_map/all_gather | solution.py:224
  10.7 549.0 %all-gather.23.cloned.1.call-start = ((), (), s32[]{:S(2)}) async-start(), calls=%async_computation.13 | async-start | bytes 2359296 | tf_op jit(solution)/shard_map/all_gather | solution.py:225
  11.2 673.6 %all-gather.25.cloned.1.call-start = ((), (), s32[]{:S(2)}) async-start(), calls=%async_computation.14 | async-start | bytes 9437184 | tf_op jit(solution)/shard_map/all_gather | solution.py:227
  12.0 797.7 %all-gather.27.cloned.1.call-start = ((), (), s32[]{:S(2)}) async-start(), calls=%async_computation.15 | async-start | bytes 9437184 | tf_op jit(solution)/shard_map/all_gather | solution.py:228
  12.7 916.6 %reduce-scatter.11.cloned.1.call-start = ((), (), s32[]{:S(2)}) async-start(), calls=%async_computation.17 | async-start | bytes 2359296 | tf_op jit(solution)/shard_map/reduce_scatter | solution.py:241
  90.7 419.5 %copy-start.45 = (pred[32]{0:T(512)(128)(4,1)}, pred[32]{0:T(512)(128)(4,1)S(1)}, u32[]{:S(2)}) copy-start(pred[32]{0:T(512)(128)(4,1)S(1)} %get-tuple-element.170) | copy-start | bytes 100
  90.8 26.9 %copy-start.14 = (f32[256,1024]{1,0:T(8,128)}, f32[256,1024]{1,0:T(8,128)S(1)}, u32[]{:S(2)}) copy-start(f32[256,1024]{1,0:T(8,128)S(1)} %bitcast_convert_fusion) | copy-start | bytes 3145732
  91.6 26.1 %copy-start.85 = (f32[256]{0:T(256)}, f32[256]{0:T(256)S(1)}, u32[]{:S(2)}) copy-start(f32[256]{0:T(256)S(1)} %fusion.63) | copy-start | bytes 3076
  91.7 26.0 %copy-start.59 = (f32[256]{0:T(256)}, f32[256]{0:T(256)S(1)}, u32[]{:S(2)}) copy-start(f32[256]{0:T(256)S(1)} %fusion.196) | copy-start | bytes 3076
  124.2 170.1 %copy-start.19 = (bf16[256,16,64]{0,2,1:T(8,128)(2,1)}, bf16[256,16,64]{0,2,1:T(8,128)(2,1)S(1)}, u32[]{:S(2)}) copy-start(bf16[256,16,64]{0,2,1:T(8,128)(2,1)S(1)} %pad_maximum_fusion) | copy-start | bytes 1572868
  163.8 130.5 %copy-start.87 = (f32[256]{0:T(256)}, f32[256]{0:T(256)S(1)}, u32[]{:S(2)}) copy-start(f32[256]{0:T(256)S(1)} %get-tuple-element.189) | copy-start | bytes 3076
  163.8 130.5 %copy-start.54 = (f32[256]{0:T(256)}, f32[256]{0:T(256)S(1)}, u32[]{:S(2)}) copy-start(f32[256]{0:T(256)S(1)} %fusion.197) | copy-start | bytes 3076
  418.6 95.9 %copy-start.23 = (f32[256,1024]{1,0:T(8,128)}, f32[256,1024]{1,0:T(8,128)S(1)}, u32[]{:S(2)}) copy-start(f32[256,1024]{1,0:T(8,128)S(1)} %convolution_add_fusion.1) | copy-start | bytes 3145732
  419.4 94.7 %copy-start.98 = (f32[32]{0:T(128)}, f32[32]{0:T(128)S(1)}, u32[]{:S(2)}) copy-start(f32[32]{0:T(128)S(1)} %multiply_reduce_fusion.13) | copy-start | bytes 388
  419.5 94.7 %copy-start.82 = (f32[32]{0:T(128)}, f32[32]{0:T(128)S(1)}, u32[]{:S(2)}) copy-start(f32[32]{0:T(128)S(1)} %fusion.201) | copy-start | bytes 388
  514.2 45.5 %copy-start.46 = (pred[32]{0:T(512)(128)(4,1)S(1)}, pred[32]{0:T(512)(128)(4,1)}, u32[]{:S(2)}) copy-start(pred[32]{0:T(512)(128)(4,1)} %copy-done.45) | copy-start | bytes 100
  514.2 48.4 %copy-start.78 = (bf16[1024,1]{0,1:T(2,128)(2,1)S(1)}, bf16[1024,1]{0,1:T(2,128)(2,1)}, u32[]{:S(2)}) copy-start(bf16[1024,1]{0,1:T(2,128)(2,1)} %reshape.478) | copy-start | bytes 6148
  516.6 173.4 %copy-start.38 = (bf16[32,1024]{1,0:T(8,128)(2,1)}, bf16[32,1024]{1,0:T(8,128)(2,1)S(1)}, u32[]{:S(2)}) copy-start(bf16[32,1024]{1,0:T(8,128)(2,1)S(1)} %convert_element_type.326) | copy-start | bytes 196612
  562.5 256.6 %copy-start.57 = (f32[32]{0:T(128)}, f32[32]{0:T(128)S(1)}, u32[]{:S(2)}) copy-start(f32[32]{0:T(128)S(1)} %fusion.202) | copy-start | bytes 388
  562.8 256.3 %copy-start.79 = (f32[32]{0:T(128)}, f32[32]{0:T(128)S(1)}, u32[]{:S(2)}) copy-start(f32[32]{0:T(128)S(1)} %fusion.60) | copy-start | bytes 388
  690.0 125.8 %copy-start.10 = (f32[32,4096]{1,0:T(8,128)}, f32[32,4096]{1,0:T(8,128)S(1)}, u32[]{:S(2)}) copy-start(f32[32,4096]{1,0:T(8,128)S(1)} %fusion.205) | copy-start | bytes 1572868
  834.4 13.3 copy-start.94
  858.2 138.1 %reduce-scatter.19.cloned.1.call-start = ((), (), s32[]{:S(2)}) async-start(), calls=%async_computation.21 | async-start | bytes 2359296 | tf_op jit(solution)/shard_map/reduce_scatter | solution.py:241
  863.3 9.7 copy-start.27
  878.8 238.1 %reduce-scatter.9.cloned.1.call-start = ((), (), s32[]{:S(2)}) async-start(), calls=%async_computation.16 | async-start | bytes 7077888 | tf_op jit(solution)/shard_map/reduce_scatter | solution.py:238
  892.8 344.9 %reduce-scatter.17.cloned.1.call-start = ((), (), s32[]{:S(2)}) async-start(), calls=%async_computation.20 | async-start | bytes 7077888 | tf_op jit(solution)/shard_map/reduce_scatter | solution.py:238
  898.2 489.9 %reduce-scatter.13.cloned.1.call-start = ((), (), s32[]{:S(2)}) async-start(), calls=%async_computation.18 | async-start | bytes 9437184 | tf_op jit(solution)/shard_map/reduce_scatter | solution.py:247
  906.2 631.9 %reduce-scatter.15.cloned.1.call-start = ((), (), s32[]{:S(2)}) async-start(), calls=%async_computation.19 | async-start | bytes 9437184 | tf_op jit(solution)/shard_map/reduce_scatter | solution.py:250
  915.9 772.3 %reduce-scatter.21.cloned.1.call-start = ((), (), s32[]{:S(2)}) async-start(), calls=%async_computation.22 | async-start | bytes 9437184 | tf_op jit(solution)/shard_map/reduce_scatter | solution.py:247
  922.5 915.7 %reduce-scatter.23.cloned.1.call-start = ((), (), s32[]{:S(2)}) async-start(), calls=%async_computation.23 | async-start | bytes 9437184 | tf_op jit(solution)/shard_map/reduce_scatter | solution.py:250
  929.2 909.0 %copy-start.105 = (u32[32]{0:T(128)S(1)}, u32[32]{0:T(128)}, u32[]{:S(2)}) copy-start(u32[32]{0:T(128)} %constant.160) | copy-start | bytes 388
  929.2 910.3 %copy-start.24 = (f32[256,1024]{1,0:T(8,128)S(1)}, f32[256,1024]{1,0:T(8,128)}, u32[]{:S(2)}) copy-start(f32[256,1024]{1,0:T(8,128)} %copy-done.23) | copy-start | bytes 3145732
  929.2 910.3 %copy-start.32 = (f32[32,1024]{1,0:T(8,128)S(1)}, f32[32,1024]{1,0:T(8,128)}, u32[]{:S(2)}) copy-start(f32[32,1024]{1,0:T(8,128)} %copy-done.31) | copy-start | bytes 393220
  929.2 911.7 %copy-start.61 = (f32[256]{0:T(256)S(1)}, f32[256]{0:T(256)}, u32[]{:S(2)}) copy-start(f32[256]{0:T(256)} %copy-done.59) | copy-start | bytes 3076
  929.3 1031.9 %all-reduce.9.cloned.1.call-start = ((), (), s32[]{:S(2)}) async-start(), calls=%async_computation.24 | async-start | bytes 12582912 | tf_op jit(solution)/shard_map/psum | solution.py:256
  1841.0 34.8 %copy-start.95 = (f32[32]{0:T(128)S(1)}, f32[32]{0:T(128)}, u32[]{:S(2)}) copy-start(f32[32]{0:T(128)} %copy-done.94) | copy-start | bytes 388
  1841.0 72.8 %copy-start.86 = (f32[256]{0:T(256)S(1)}, f32[256]{0:T(256)}, u32[]{:S(2)}) copy-start(f32[256]{0:T(256)} %copy-done.85) | copy-start | bytes 3076
  (77 other events, 288.9 us)
Sparse Core Ops, SparseCore 0:
  10.3 101.5 all-gather.12
  114.0 47.3 all-gather.14
  163.5 122.9 all-gather.16
  288.5 122.6 all-gather.18
  413.2 96.8 all-gather.20
  512.1 47.4 all-gather.22
  561.8 122.9 all-gather.24
  687.0 122.6 all-gather.26
  858.3 66.6 reduce-scatter.10
  928.9 67.2 reduce-scatter.18
  999.8 117.0 reduce-scatter.8
  1120.4 117.2 reduce-scatter.16
  1241.3 146.6 reduce-scatter.12
  1391.5 146.5 reduce-scatter.14
  1541.6 146.5 reduce-scatter.20
  1691.6 146.5 reduce-scatter.22
  1840.9 120.1 all-reduce.8
where the time goes:
time: 1990 us; the launch traced here: 1980 us
  waiting for transfers between devices  1630 us (82%)
  matrix products  143 us (7%)
  blocking collectives  139 us (7%)
  other arithmetic  35.4 us (2%)
    reduce_scatter x2, waiting for transfers between devices, reduce_grads(): lax.psum_scatter(upward.astype(jnp.bfloat16), 'wide', scatter_dimension=0...  300 us
    reduce_scatter x2, waiting for transfers between devices, reduce_grads(): lax.psum_scatter(downward.astype(jnp.bfloat16), 'wide', scatter_dimension...  300 us
    all_gather x2, waiting for transfers between devices, fetch_weights(): lax.all_gather(upward, 'wide', axis=0, tiled=True)  245 us
    reduce_scatter x2, waiting for transfers between devices, reduce_grads(): lax.psum_scatter(mixing.astype(jnp.bfloat16), 'wide', scatter_dimension=0...  241 us
    all_gather x2, waiting for transfers between devices, fetch_weights(): lax.all_gather(downward, 'wide', axis=0, tiled=True)  237 us
    all_gather x2, waiting for transfers between devices, fetch_weights(): lax.all_gather(mixing, 'wide', axis=0, tiled=True)  110 us
    all_gather x2, waiting for transfers between devices, fetch_weights(): lax.all_gather(project, 'wide', axis=0, tiled=True)  80.2 us
    reduce_scatter x2, waiting for transfers between devices, reduce_grads(): lax.psum_scatter(project.astype(jnp.bfloat16), 'wide', scatter_dimension=...  66.9 us
  transfers between devices with their start and end apart: 17, of which 16 were waited for; matrix products, arithmetic and copies ran while one was open for 6% of the time, Pallas kernels for 0%

commit v1 on v0

--- a/solution.py
+++ b/solution.py
@@ -1,3 +1,4 @@
+import functools
 import jax
 import jax.numpy as jnp
 from jax import lax
@@ -8,6 +9,28 @@
 NEG = -1e30
 HIGH = lax.Precision.HIGHEST
 GROUP_HEADS = 4
+
+
+def cover_matrix(content, bus_axis):
+    built, y2, all_values = (lax.axis_size(bus_axis), lax.axis_index(bus_axis), content.shape[0])
+    f_next, piece_out = (content, 1)
+    while piece_out < built:
+        f_next = jnp.concatenate(
+            [
+                f_next,
+                lax.ppermute(
+                    f_next,
+                    axis_name=bus_axis,
+                    perm=[(dev_j, (dev_j - piece_out) % built) for dev_j in range(built)],
+                ),
+            ],
+            axis=0,
+        )
+        piece_out = 2 * piece_out
+    return jnp.roll(f_next, y2 * all_values, axis=0)
+
+
+resolve_lines = functools.partial(cover_matrix, bus_axis="wide")
 
 
 def rms_norm(values, gain):
@@ -225,7 +248,7 @@
         lax.all_gather(project, "wide", axis=0, tiled=True),
         lax.all_gather(feed_gain, "wide", axis=0, tiled=True),
         lax.all_gather(upward, "wide", axis=0, tiled=True),
-        lax.all_gather(downward, "wide", axis=0, tiled=True),
+        resolve_lines(downward),
     )
 
 

time: 1990 us -> 2230 us (1.12)
  blocking collectives: 139 us -> 407 us
  waiting for transfers between devices: 1630 us -> 1380 us
  starting transfers between devices: 1.06 us -> 104 us
  other arithmetic: 35.4 us -> 136 us
    all_gather x2 -> x0, waiting for transfers between devices: 237 us -> none  [fetch_weights(): lax.all_gather(downward, 'wide', axis=0, tiled=True)]
    ppermute x0 -> x6, waiting for transfers between devices: none -> 196 us  [cover_matrix(): lax.ppermute(f_next, axis_name=bus_axis, perm=[(dev_j, (dev_j - piece_out...]
    all_gather x2, blocking collectives: 33.8 us -> 214 us  [fetch_weights(): lax.all_gather(feed_gain, 'wide', axis=0, tiled=True)]
    all_gather x2, waiting for transfers between devices: 245 us -> 120 us  [fetch_weights(): lax.all_gather(upward, 'wide', axis=0, tiled=True)]
    ppermute x0 -> x6, starting transfers between devices: none -> 103 us  [cover_matrix(): lax.ppermute(f_next, axis_name=bus_axis, perm=[(dev_j, (dev_j - piece_out...]
    concatenate x0 -> x6, other arithmetic: none -> 92.3 us  [the longest x2 80.9 us: cover_matrix(): return jnp.roll(f_next, y2 * all_values, axis=0)]
    all_gather x2, blocking collectives: 41.6 us -> 129 us  [fetch_weights(): lax.all_gather(attn_gain, 'wide', axis=0, tiled=True)]
    all_gather x2, waiting for transfers between devices: 80.2 us -> 38.5 us  [fetch_weights(): lax.all_gather(project, 'wide', axis=0, tiled=True)]
  transfers between devices with their start and end apart: 17 -> 21, of which waited for: 16 -> 14; matrix products, arithmetic and copies ran while one was open for 6% -> 10% of each run, Pallas kernels for 0% -> 0%
where the time goes in v1:
time: 2230 us; the launch traced here: 2220 us
  waiting for transfers between devices  1380 us (62%)
  blocking collectives  407 us (18%)
  matrix products  156 us (7%)
  other arithmetic  136 us (6%)
  starting transfers between devices  104 us (5%)
    reduce_scatter x2, waiting for transfers between devices, reduce_grads(): lax.psum_scatter(upward.astype(jnp.bfloat16), 'wide', scatter_dimension=0...  301 us
    reduce_scatter x2, waiting for transfers between devices, reduce_grads(): lax.psum_scatter(downward.astype(jnp.bfloat16), 'wide', scatter_dimension...  300 us
    reduce_scatter x2, waiting for transfers between devices, reduce_grads(): lax.psum_scatter(mixing.astype(jnp.bfloat16), 'wide', scatter_dimension=0...  241 us
    all_gather x2, blocking collectives, fetch_weights(): lax.all_gather(feed_gain, 'wide', axis=0, tiled=True)  214 us
    ppermute x6, waiting for transfers between devices, cover_matrix(): lax.ppermute(f_next, axis_name=bus_axis, perm=[(dev_j, (dev_j - piece_out...  196 us
    all_gather x2, blocking collectives, fetch_weights(): lax.all_gather(attn_gain, 'wide', axis=0, tiled=True)  129 us
    all_gather x2, waiting for transfers between devices, fetch_weights(): lax.all_gather(upward, 'wide', axis=0, tiled=True)  120 us
    ppermute x6, starting transfers between devices, cover_matrix(): lax.ppermute(f_next, axis_name=bus_axis, perm=[(dev_j, (dev_j - piece_out...  103 us
  transfers between devices with their start and end apart: 21, of which 14 were waited for; matrix products, arithmetic and copies ran while one was open for 10% of the time, Pallas kernels for 0%

profile of v1, /device:TPU:0, one launch (start us, length us, event | category | flops | bytes accessed | tf_op | source)
XLA Modules:
  0.0 2221.3 jit_solution(17155097160085508881)
XLA Ops:
  10.0 6.1 collective-permute-start
  16.1 40.6 %collective-permute-done = bf16[512,1024]{1,0:T(8,128)(2,1)S(1)} collective-permute-done((bf16[512,1024]{1,0:T(8,128)(2,1)}, bf16[512,1024]{1,0:T(8,128)(2,1)S(1)}, u32[]{:S(2)}, u32[]{:S(2)}) %collective-permute-start) | collective-permute-done | bytes 1048608 | tf_op jit(solution)/shard_map/ppermute | solution.py:21
  60.6 5.1 collective-permute-start.3
  65.7 65.8 %collective-permute-done.3 = bf16[512,1024]{1,0:T(8,128)(2,1)S(1)} collective-permute-done((bf16[512,1024]{1,0:T(8,128)(2,1)S(1)}, bf16[512,1024]{1,0:T(8,128)(2,1)S(1)}, u32[]{:S(2)}, u32[]{:S(2)}) %collective-permute-start.3) | collective-permute-done | bytes 1048608 | tf_op jit(solution)/shard_map/ppermute | solution.py:21
  133.6 3.5 pad_maximum_fusion
  139.1 89.2 %collective-permute-done.4 = bf16[1024,1024]{1,0:T(8,128)(2,1)} collective-permute-done((bf16[1024,1024]{1,0:T(8,128)(2,1)}, bf16[1024,1024]{1,0:T(8,128)(2,1)}, u32[]{:S(2)}, u32[]{:S(2)}) %collective-permute-start.4) | collective-permute-done | bytes 2097184 | tf_op jit(solution)/shard_map/ppermute | solution.py:21
  228.3 3.6 pad_maximum_fusion.1
  231.9 89.6 %collective-permute-start.5 = (bf16[2048,1024]{1,0:T(8,128)(2,1)}, bf16[2048,1024]{1,0:T(8,128)(2,1)}, u32[]{:S(2)}, u32[]{:S(2)}) collective-permute-start(bf16[2048,1024]{1,0:T(8,128)(2,1)} %pad_maximum_fusion.1), channel_id=1, source_target_pairs={{0,16},{4,20},{8,24},{12,28},{16,0},{20,4},{24,8},{28,12},{1,17},{... | collective-permute-start | bytes 12582920 | tf_op jit(solution)/shard_map/ppermute | solution.py:21
  322.7 112.8 %all-gather = bf16[8,1,128]{2,1,0:T(2,128)(2,1)S(1)} all-gather(bf16[1,1,128]{2,1,0:T(2,128)(2,1)S(1)} %bitcast.330), channel_id=1, replica_groups=mesh['wide'=8,'narrow'=4] {'wide'}, dimensions={0}, use_global_device_ids=true | all-gather | bytes 2304 | tf_op jit(solution)/shard_map/all_gather | solution.py:246
  435.5 194.5 %all-gather.1 = bf16[8,1,128]{2,1,0:T(2,128)(2,1)S(1)} all-gather(bf16[1,1,128]{2,1,0:T(2,128)(2,1)S(1)} %bitcast.331), channel_id=1, replica_groups=mesh['wide'=8,'narrow'=4] {'wide'}, dimensions={0}, use_global_device_ids=true | all-gather | bytes 2304 | tf_op jit(solution)/shard_map/all_gather | solution.py:249
  630.0 16.3 all-gather.2
  646.3 19.4 all-gather.3
  668.2 35.1 %fusion.10 = bf16[4096,1024]{1,0:T(8,128)(2,1)} fusion(s32[]{:T(128)S(6)} %select_n.115, bf16[512,1024]{1,0:T(8,128)(2,1)S(1)} %copy-done.16, bf16[512,1024]{1,0:T(8,128)(2,1)} %copy-done.19, bf16[1024,1024]{1,0:T(8,128)(2,1)} %collective-permute-done.1, bf16[2048,1024]{1,0:T(8,128)(2,1)} %collective-permute-done.2), kind=kLoop, calls=%fused_computation.31 | loop fusion | flops 67108864 | bytes 16777220 | tf_op jit(solution)/shard_map/jit(_roll_dynamic)/concatenate | solution.py:30
  703.4 45.8 %fusion.3 = bf16[4096,1024]{1,0:T(8,128)(2,1)} fusion(s32[]{:T(128)S(6)} %select_n.115, bf16[512,1024]{1,0:T(8,128)(2,1)S(1)} %copy-done.18, bf16[512,1024]{1,0:T(8,128)(2,1)S(1)} %copy-done.22, bf16[1024,1024]{1,0:T(8,128)(2,1)} %collective-permute-done.4, bf16[2048,1024]{1,0:T(8,128)(2,1)} %collective-permute-done.5), kind=kLoop, calls=%fused_computation.24 | loop fusion | flops 67108864 | bytes 16777220 | tf_op jit(solution)/shard_map/jit(_roll_dynamic)/concatenate | solution.py:30
  749.2 5.8 convolution_convert_fusion.6
  764.1 6.0 fusion.225
  772.2 6.2 convolution_add_fusion.1
  779.2 75.0 %all-gather.17.cloned.1.call-done = bf16[1024,3072]{1,0:T(8,128)(2,1)} async-done(((bf16[128,3072]{1,0:T(8,128)(2,1)}), bf16[1024,3072]{1,0:T(8,128)(2,1)}) %all-gather.17.cloned.1.call-update) | async-done | bytes 6291472 | tf_op jit(solution)/shard_map/all_gather | solution.py:247
  854.2 4.7 convolution_convert_fusion.7
  865.0 38.5 %all-gather.19.cloned.1.call-done = bf16[1024,1024]{1,0:T(8,128)(2,1)} async-done(((bf16[128,1024]{1,0:T(8,128)(2,1)}), bf16[1024,1024]{1,0:T(8,128)(2,1)}) %all-gather.19.cloned.1.call-update) | async-done | bytes 2097168 | tf_op jit(solution)/shard_map/all_gather | solution.py:248
  909.0 119.5 %all-gather.21.cloned.1.call-done = bf16[1024,4096]{1,0:T(8,128)(2,1)} async-done(((bf16[128,4096]{1,0:T(8,128)(2,1)}), bf16[1024,4096]{1,0:T(8,128)(2,1)}) %all-gather.21.cloned.1.call-update) | async-done | bytes 8388624 | tf_op jit(solution)/shard_map/all_gather | solution.py:250
  1028.5 5.2 fusion.219
  1033.7 6.2 fusion.98
  1040.0 3.1 multiply_reduce_fusion.7
  1057.0 5.6 convolution_add_fusion.2
  1065.7 6.0 multiply_reduce_fusion.8
  1074.7 11.6 fusion.20
  1086.4 7.3 multiply_reduce_fusion
  1102.4 3.2 convolution_convert_fusion.10
  1118.2 3.2 multiply_reduce_fusion.2
  1131.8 4.6 convolution_convert_fusion.5
  1136.4 5.5 convolution_convert_fusion.4
  1142.6 7.3 convolution_convert_fusion.3
  1151.1 8.4 convolution_convert_fusion.2
  1160.5 5.7 convolution_convert_fusion.1
  1166.8 5.6 convolution_convert_fusion
  1172.6 62.9 %reduce-scatter.19.cloned.1.call-done = bf16[128,1024]{1,0:T(8,128)(2,1)} async-done(((bf16[1024,1024]{1,0:T(8,128)(2,1)}), bf16[128,1024]{1,0:T(8,128)(2,1)}) %reduce-scatter.19.cloned.1.call-update) | async-done | bytes 262160 | tf_op jit(solution)/shard_map/reduce_scatter | solution.py:264
  1235.5 120.6 %reduce-scatter.9.cloned.1.call-done = bf16[128,3072]{1,0:T(8,128)(2,1)} async-done(((bf16[1024,3072]{1,0:T(8,128)(2,1)}), bf16[128,3072]{1,0:T(8,128)(2,1)}) %reduce-scatter.9.cloned.1.call-update) | async-done | bytes 786448 | tf_op jit(solution)/shard_map/reduce_scatter | solution.py:261
  1356.2 120.7 %reduce-scatter.17.cloned.1.call-done = bf16[128,3072]{1,0:T(8,128)(2,1)} async-done(((bf16[1024,3072]{1,0:T(8,128)(2,1)}), bf16[128,3072]{1,0:T(8,128)(2,1)}) %reduce-scatter.17.cloned.1.call-update) | async-done | bytes 786448 | tf_op jit(solution)/shard_map/reduce_scatter | solution.py:261
  1476.9 150.4 %reduce-scatter.13.cloned.1.call-done = bf16[128,4096]{1,0:T(8,128)(2,1)} async-done(((bf16[1024,4096]{1,0:T(8,128)(2,1)}), bf16[128,4096]{1,0:T(8,128)(2,1)}) %reduce-scatter.13.cloned.1.call-update) | async-done | bytes 1048592 | tf_op jit(solution)/shard_map/reduce_scatter | solution.py:270
  1627.3 150.1 %reduce-scatter.15.cloned.1.call-done = bf16[512,1024]{1,0:T(8,128)(2,1)} async-done(((bf16[4096,1024]{1,0:T(8,128)(2,1)}), bf16[512,1024]{1,0:T(8,128)(2,1)}) %reduce-scatter.15.cloned.1.call-update) | async-done | bytes 1048592 | tf_op jit(solution)/shard_map/reduce_scatter | solution.py:273
  1777.4 150.2 %reduce-scatter.21.cloned.1.call-done = bf16[128,4096]{1,0:T(8,128)(2,1)} async-done(((bf16[1024,4096]{1,0:T(8,128)(2,1)}), bf16[128,4096]{1,0:T(8,128)(2,1)}) %reduce-scatter.21.cloned.1.call-update) | async-done | bytes 1048592 | tf_op jit(solution)/shard_map/reduce_scatter | solution.py:270
  1927.6 150.1 %reduce-scatter.23.cloned.1.call-done = bf16[512,1024]{1,0:T(8,128)(2,1)} async-done(((bf16[4096,1024]{1,0:T(8,128)(2,1)}), bf16[512,1024]{1,0:T(8,128)(2,1)}) %reduce-scatter.23.cloned.1.call-update) | async-done | bytes 1048592 | tf_op jit(solution)/shard_map/reduce_scatter | solution.py:273
  2080.5 6.2 fusion.76
  2086.7 19.7 all-reduce.4
  2106.7 6.5 all-reduce.5
  2115.5 37.8 %psum.103 = f32[1024]{0:T(1024)} all-reduce(f32[1024]{0:T(1024)S(1)} %bitcast.328), channel_id=1, replica_groups=mesh['wide'=8,'narrow'=4] {'wide','narrow'}, use_global_device_ids=true, to_apply=%region_63.66 | all-reduce | flops 1024 | bytes 8192 | tf_op jit(solution)/shard_map/psum | solution.py:370
  2156.5 44.0 %all-reduce.9.cloned.1.call-done = (bf16[128,3072]{1,0:T(8,128)(2,1)}, bf16[128,1024]{1,0:T(8,128)(2,1)}, bf16[128,4096]{1,0:T(8,128)(2,1)}, bf16[512,1024]{1,0:...) async-done(((bf16[128,3072]{1,0:T(8,128)(2,1)}, bf16[128,1024]{1,0:T(8,128)(2,1)}, ...) | async-done | bytes 6291472 | tf_op jit(solution)/shard_map/psum | solution.py:279
  (384 shorter events, 114.5 us)
Async XLA Ops:
  7.2 53.4 %copy-start.17 = (bf16[512,1024]{1,0:T(8,128)(2,1)S(1)}, bf16[512,1024]{1,0:T(8,128)(2,1)}, u32[]{:S(2)}) copy-start(bf16[512,1024]{1,0:T(8,128)(2,1)} %param.36) | copy-start | bytes 3145732
  7.2 742.0 %all-gather.11.cloned.1.call-start = ((), (), s32[]{:S(2)}) async-start(), calls=%async_computation.8 | async-start | bytes 7077888 | tf_op jit(solution)/shard_map/all_gather | solution.py:247
  7.9 753.6 %all-gather.13.cloned.1.call-start = ((), (), s32[]{:S(2)}) async-start(), calls=%async_computation.9 | async-start | bytes 2359296 | tf_op jit(solution)/shard_map/all_gather | solution.py:248
  8.7 755.5 %all-gather.15.cloned.1.call-start = ((), (), s32[]{:S(2)}) async-start(), calls=%async_computation.10 | async-start | bytes 9437184 | tf_op jit(solution)/shard_map/all_gather | solution.py:250
  9.4 844.8 %all-gather.17.cloned.1.call-start = ((), (), s32[]{:S(2)}) async-start(), calls=%async_computation.11 | async-start | bytes 7077888 | tf_op jit(solution)/shard_map/all_gather | solution.py:247
  10.0 123.6 %copy-start.16 = (bf16[512,1024]{1,0:T(8,128)(2,1)S(1)}, bf16[512,1024]{1,0:T(8,128)(2,1)}, u32[]{:S(2)}) copy-start(bf16[512,1024]{1,0:T(8,128)(2,1)} %param.30) | copy-start | bytes 3145732
  10.0 893.5 %all-gather.19.cloned.1.call-start = ((), (), s32[]{:S(2)}) async-start(), calls=%async_computation.12 | async-start | bytes 2359296 | tf_op jit(solution)/shard_map/all_gather | solution.py:248
  10.0 46.6 %collective-permute-start = (bf16[512,1024]{1,0:T(8,128)(2,1)}, bf16[512,1024]{1,0:T(8,128)(2,1)S(1)}, u32[]{:S(2)}, u32[]{:S(2)}) collective-permute-start(bf16[512,1024]{1,0:T(8,128)(2,1)} %param.30), channel_id=1, source_target_pairs={{0,28},{4,0},{8,4},{12,8},{16,12},{20,16},{24,20},{28,24},{1,29},{... | collective-permute-start | bytes 3145736 | tf_op jit(solution)/shard_map/ppermute | solution.py:21
  60.5 73.2 %collective-permute-start.1 = (bf16[1024,1024]{1,0:T(8,128)(2,1)}, bf16[1024,1024]{1,0:T(8,128)(2,1)}, u32[]{:S(2)}, u32[]{:S(2)}) collective-permute-start(bf16[1024,1024]{1,0:T(8,128)(2,1)} %pad_maximum_fusion.2), channel_id=1, source_target_pairs={{0,24},{4,28},{8,0},{12,4},{16,8},{20,12},{24,16},{28,20},{1,25},{... | collective-permute-start | bytes 6291464 | tf_op jit(solution)/shard_map/ppermute | solution.py:21
  60.5 968.0 %all-gather.21.cloned.1.call-start = ((), (), s32[]{:S(2)}) async-start(), calls=%async_computation.13 | async-start | bytes 9437184 | tf_op jit(solution)/shard_map/all_gather | solution.py:250
  60.6 73.1 %copy-start.20 = (bf16[512,1024]{1,0:T(8,128)(2,1)S(1)}, bf16[512,1024]{1,0:T(8,128)(2,1)}, u32[]{:S(2)}) copy-start(bf16[512,1024]{1,0:T(8,128)(2,1)} %copy-done.19) | copy-start | bytes 3145732
  60.6 70.9 %collective-permute-start.3 = (bf16[512,1024]{1,0:T(8,128)(2,1)S(1)}, bf16[512,1024]{1,0:T(8,128)(2,1)S(1)}, u32[]{:S(2)}, u32[]{:S(2)}) collective-permute-start(bf16[512,1024]{1,0:T(8,128)(2,1)S(1)} %copy-done.17), channel_id=1, source_target_pairs={{0,28},{4,0},{8,4},{12,8},{16,12},{20,16},{24,20},{28,24},{1,29},{... | collective-permute-start | bytes 3145736 | tf_op jit(solution)/shard_map/ppermute | solution.py:21
  133.1 95.2 %collective-permute-start.4 = (bf16[1024,1024]{1,0:T(8,128)(2,1)}, bf16[1024,1024]{1,0:T(8,128)(2,1)}, u32[]{:S(2)}, u32[]{:S(2)}) collective-permute-start(bf16[1024,1024]{1,0:T(8,128)(2,1)} %pad_maximum_fusion.3), channel_id=1, source_target_pairs={{0,24},{4,28},{8,0},{12,4},{16,8},{20,12},{24,16},{28,20},{1,25},{... | collective-permute-start | bytes 6291464 | tf_op jit(solution)/shard_map/ppermute | solution.py:21
  137.1 531.1 %collective-permute-start.2 = (bf16[2048,1024]{1,0:T(8,128)(2,1)}, bf16[2048,1024]{1,0:T(8,128)(2,1)}, u32[]{:S(2)}, u32[]{:S(2)}) collective-permute-start(bf16[2048,1024]{1,0:T(8,128)(2,1)} %pad_maximum_fusion), channel_id=1, source_target_pairs={{0,16},{4,20},{8,24},{12,28},{16,0},{20,4},{24,8},{28,12},{1,17},{... | collective-permute-start | bytes 12582920 | tf_op jit(solution)/shard_map/ppermute | solution.py:21
  138.9 182.5 %copy-start.83 = (s32[1,32]{1,0:T(1,128)S(1)}, s32[1,32]{1,0:T(1,128)}, u32[]{:S(2)}) copy-start(s32[1,32]{1,0:T(1,128)} %param.23) | copy-start | bytes 388
  139.0 182.5 %copy-start.82 = (bf16[1024]{0:T(1024)(128)(2,1)S(1)}, bf16[1024]{0:T(1024)(128)(2,1)}, u32[]{:S(2)}) copy-start(bf16[1024]{0:T(1024)(128)(2,1)} %param.37) | copy-start | bytes 6148
  139.0 183.7 %copy-start.89 = (bf16[128]{0:T(256)(128)(2,1)S(1)}, bf16[128]{0:T(256)(128)(2,1)}, u32[]{:S(2)}) copy-start(bf16[128]{0:T(256)(128)(2,1)} %param.25) | copy-start | bytes 772
  139.0 296.5 %copy-start.90 = (bf16[128]{0:T(256)(128)(2,1)S(1)}, bf16[128]{0:T(256)(128)(2,1)}, u32[]{:S(2)}) copy-start(bf16[128]{0:T(256)(128)(2,1)} %param.28) | copy-start | bytes 772
  139.0 491.0 %copy-start.91 = (bf16[128]{0:T(256)(128)(2,1)S(1)}, bf16[128]{0:T(256)(128)(2,1)}, u32[]{:S(2)}) copy-start(bf16[128]{0:T(256)(128)(2,1)} %param.31) | copy-start | bytes 772
  139.0 507.3 %copy-start.92 = (bf16[128]{0:T(256)(128)(2,1)S(1)}, bf16[128]{0:T(256)(128)(2,1)}, u32[]{:S(2)}) copy-start(bf16[128]{0:T(256)(128)(2,1)} %param.34) | copy-start | bytes 772
  139.0 526.7 %copy-start = (s32[1,256]{1,0:T(1,128)S(1)}, s32[1,256]{1,0:T(1,128)}, u32[]{:S(2)}) copy-start(s32[1,256]{1,0:T(1,128)} %param.22) | copy-start | bytes 3076
  139.0 527.4 %copy-start.46 = (bf16[1,256,1024]{2,1,0:T(8,128)(2,1)S(1)}, bf16[1,256,1024]{2,1,0:T(8,128)(2,1)}, u32[]{:S(2)}) copy-start(bf16[1,256,1024]{2,1,0:T(8,128)(2,1)} %param.24) | copy-start | bytes 1572868
  139.0 528.1 %copy-start.10 = (bf16[1,256,1024]{2,1,0:T(8,128)(2,1)S(1)}, bf16[1,256,1024]{2,1,0:T(8,128)(2,1)}, u32[]{:S(2)}) copy-start(bf16[1,256,1024]{2,1,0:T(8,128)(2,1)} %param.21) | copy-start | bytes 1572868
  139.1 1033.6 %reduce-scatter.11.cloned.1.call-start = ((), (), s32[]{:S(2)}) async-start(), calls=%async_computation.15 | async-start | bytes 2359296 | tf_op jit(solution)/shard_map/reduce_scatter | solution.py:264
  231.9 471.5 %collective-permute-start.5 = (bf16[2048,1024]{1,0:T(8,128)(2,1)}, bf16[2048,1024]{1,0:T(8,128)(2,1)}, u32[]{:S(2)}, u32[]{:S(2)}) collective-permute-start(bf16[2048,1024]{1,0:T(8,128)(2,1)} %pad_maximum_fusion.1), channel_id=1, source_target_pairs={{0,16},{4,20},{8,24},{12,28},{16,0},{20,4},{24,8},{28,12},{1,17},{... | collective-permute-start | bytes 12582920 | tf_op jit(solution)/shard_map/ppermute | solution.py:21
  321.5 381.9 %copy-start.93 = (s32[32]{0:T(128)}, s32[32]{0:T(128)S(1)}, u32[]{:S(2)}) copy-start(s32[32]{0:T(128)S(1)} %fusion.212) | copy-start | bytes 388
  666.4 187.8 %copy-start.49 = (pred[32]{0:T(512)(128)(4,1)}, pred[32]{0:T(512)(128)(4,1)S(1)}, u32[]{:S(2)}) copy-start(pred[32]{0:T(512)(128)(4,1)S(1)} %get-tuple-element.171) | copy-start | bytes 100
  667.4 81.8 %copy-start.61 = (f32[256]{0:T(256)}, f32[256]{0:T(256)S(1)}, u32[]{:S(2)}) copy-start(f32[256]{0:T(256)S(1)} %fusion.210) | copy-start | bytes 3076
  778.3 81.8 %copy-start.28 = (f32[256,1024]{1,0:T(8,128)}, f32[256,1024]{1,0:T(8,128)S(1)}, u32[]{:S(2)}) copy-start(f32[256,1024]{1,0:T(8,128)S(1)} %convolution_add_fusion.1) | copy-start | bytes 3145732
  779.1 79.7 %copy-start.87 = (f32[32]{0:T(128)}, f32[32]{0:T(128)S(1)}, u32[]{:S(2)}) copy-start(f32[32]{0:T(128)S(1)} %multiply_reduce_fusion.13) | copy-start | bytes 388
  779.2 79.7 %copy-start.75 = (f32[32]{0:T(128)}, f32[32]{0:T(128)S(1)}, u32[]{:S(2)}) copy-start(f32[32]{0:T(128)S(1)} %fusion.215) | copy-start | bytes 388
  860.2 47.9 %copy-start.50 = (pred[32]{0:T(512)(128)(4,1)S(1)}, pred[32]{0:T(512)(128)(4,1)}, u32[]{:S(2)}) copy-start(pred[32]{0:T(512)(128)(4,1)} %copy-done.49) | copy-start | bytes 100
  865.0 168.7 %copy-start.42 = (bf16[32,1024]{1,0:T(8,128)(2,1)}, bf16[32,1024]{1,0:T(8,128)(2,1)S(1)}, u32[]{:S(2)}) copy-start(bf16[32,1024]{1,0:T(8,128)(2,1)S(1)} %convert_element_type.326) | copy-start | bytes 196612
  905.7 137.4 %copy-start.59 = (f32[32]{0:T(128)}, f32[32]{0:T(128)S(1)}, u32[]{:S(2)}) copy-start(f32[32]{0:T(128)S(1)} %fusion.216) | copy-start | bytes 388
  909.0 134.1 %copy-start.72 = (f32[32]{0:T(128)}, f32[32]{0:T(128)S(1)}, u32[]{:S(2)}) copy-start(f32[32]{0:T(128)S(1)} %fusion.74) | copy-start | bytes 388
  1097.3 138.3 %reduce-scatter.19.cloned.1.call-start = ((), (), s32[]{:S(2)}) async-start(), calls=%async_computation.19 | async-start | bytes 2359296 | tf_op jit(solution)/shard_map/reduce_scatter | solution.py:264
  1122.5 233.7 %reduce-scatter.9.cloned.1.call-start = ((), (), s32[]{:S(2)}) async-start(), calls=%async_computation.14 | async-start | bytes 7077888 | tf_op jit(solution)/shard_map/reduce_scatter | solution.py:261
  1136.4 340.5 %reduce-scatter.17.cloned.1.call-start = ((), (), s32[]{:S(2)}) async-start(), calls=%async_computation.18 | async-start | bytes 7077888 | tf_op jit(solution)/shard_map/reduce_scatter | solution.py:261
  1141.9 485.4 %reduce-scatter.13.cloned.1.call-start = ((), (), s32[]{:S(2)}) async-start(), calls=%async_computation.16 | async-start | bytes 9437184 | tf_op jit(solution)/shard_map/reduce_scatter | solution.py:270
  1149.9 627.5 %reduce-scatter.15.cloned.1.call-start = ((), (), s32[]{:S(2)}) async-start(), calls=%async_computation.17 | async-start | bytes 9437184 | tf_op jit(solution)/shard_map/reduce_scatter | solution.py:273
  1159.5 768.1 %reduce-scatter.21.cloned.1.call-start = ((), (), s32[]{:S(2)}) async-start(), calls=%async_computation.20 | async-start | bytes 9437184 | tf_op jit(solution)/shard_map/reduce_scatter | solution.py:270
  1166.2 911.5 %reduce-scatter.23.cloned.1.call-start = ((), (), s32[]{:S(2)}) async-start(), calls=%async_computation.21 | async-start | bytes 9437184 | tf_op jit(solution)/shard_map/reduce_scatter | solution.py:273
  1172.5 905.2 %copy-start.94 = (u32[32]{0:T(128)S(1)}, u32[32]{0:T(128)}, u32[]{:S(2)}) copy-start(u32[32]{0:T(128)} %constant.185) | copy-start | bytes 388
  1172.5 906.4 %copy-start.29 = (f32[256,1024]{1,0:T(8,128)S(1)}, f32[256,1024]{1,0:T(8,128)}, u32[]{:S(2)}) copy-start(f32[256,1024]{1,0:T(8,128)} %copy-done.28) | copy-start | bytes 3145732
  1172.5 906.4 %copy-start.36 = (f32[32,1024]{1,0:T(8,128)S(1)}, f32[32,1024]{1,0:T(8,128)}, u32[]{:S(2)}) copy-start(f32[32,1024]{1,0:T(8,128)} %convolution_add_fusion.2) | copy-start | bytes 393220
  1172.5 907.9 %copy-start.63 = (f32[256]{0:T(256)S(1)}, f32[256]{0:T(256)}, u32[]{:S(2)}) copy-start(f32[256]{0:T(256)} %copy-done.61) | copy-start | bytes 3076
  1172.5 1028.0 %all-reduce.9.cloned.1.call-start = ((), (), s32[]{:S(2)}) async-start(), calls=%async_computation.22 | async-start | bytes 12582912 | tf_op jit(solution)/shard_map/psum | solution.py:279
  2080.5 72.8 %copy-start.77 = (f32[256]{0:T(256)S(1)}, f32[256]{0:T(256)}, u32[]{:S(2)}) copy-start(f32[256]{0:T(256)} %copy-done.76) | copy-start | bytes 3076
  (68 other events, 472.5 us)
Sparse Core Ops, SparseCore 0:
  10.2 300.2 all-gather.10
  312.6 317.3 all-gather.12
  632.2 123.0 all-gather.14
  757.3 96.8 all-gather.16
  856.2 47.3 all-gather.18
  905.5 122.9 all-gather.20
  1097.4 66.6 reduce-scatter.10
  1168.1 67.3 reduce-scatter.18
  1239.1 116.9 reduce-scatter.8
  1359.6 117.2 reduce-scatter.16
  1480.5 146.7 reduce-scatter.12
  1630.8 146.5 reduce-scatter.14
  1781.0 146.5 reduce-scatter.20
  1931.1 146.5 reduce-scatter.22
  2080.4 120.1 all-reduce.8
